TPU v7x, 32 devices: a whole 2x2x4 slice. The times are simulated.
32 devices in a mesh: mesh: 8 (over y, x, core), band: 4 (over z).
Axes of the slice: x: 2, y: 2, z: 4, core: 2. Of those that a mesh axis runs over, the one named last changes fastest.
Arguments:
- states: float32 [2, 64, 8192], P(None, 'band', 'mesh'), may hold values from -6 to 6
- frozen: float32 [2, 32, 8192], P(None, 'band', 'mesh'), may hold values from -0.125 to 0.125
- weights: float32 [8, 8192], P(None, 'mesh'), may hold values from 0.1 to 1
- potential: float32 [8192], P('mesh'), may hold values from -2 to 2
- send_list: int32 [8, 8, 256], P('mesh'), may hold values from 0 to 1023
- neighbours: int32 [8, 8192], P(None, 'mesh'), may hold values from 0 to 3071, as said below
Outputs:
- evolved: float32 [2, 64, 8192], P(None, 'band', 'mesh')
Inputs may be any that keep to these rules, and one draw needn't show every extreme that they name: `neighbours`: an entry below 1024 names a point of the same part; an entry 1024 + s * 256 + c names ghost slot c from part s, where part s is at most 3 parts away in the cyclic order of parts or exactly half the number of parts away, and every part names ghost slots from all those parts. Slots of send_list[s, i] that part i never names hold arbitrary points of part s.
All inputs are finite; a program needn't handle non-finite values.
Results may differ from a plain program's by a relative error of at most 0.0001.
Values sent between devices are 32-bit elements; how exact they have to be, the bound alone decides.
No kernel may reach another device: no remote copies, remote signals or barrier semaphores. Data moves between devices by JAX's collectives and lax.ppermute only.
A program may use at most 128 MiB of HBM per device.

v0:
```python
import jax
import jax.numpy as jnp
from jax import lax
from jax.sharding import PartitionSpec as P

NBRS = 8
TERMS = 4
time_step = 0.3


def rotate(field):
    return jnp.stack([field[1], -field[0]])


def body(states, frozen, weights, potential, send_list, neighbours):
    parts = lax.axis_size("mesh")
    rows = states.shape[1]
    capacity = send_list.shape[2]
    routes = send_list[0]
    full_frozen = lax.all_gather(frozen, "band", axis=1, tiled=True)
    total = states
    term = states
    for order in range(1, TERMS + 1):
        paired = jnp.stack([term, rotate(term)])
        partial_intersection = jnp.einsum(
            "cmp,ocjp->omj", full_frozen, paired, precision=lax.Precision.HIGHEST
        )
        intersection = lax.psum(partial_intersection, "mesh")
        packed = jnp.take(term, routes.reshape(-1), axis=2).reshape(2, rows, parts, capacity)
        arrived = lax.all_to_all(packed, "mesh", split_axis=2, concat_axis=2, tiled=True)
        extended = jnp.concatenate([term, arrived.reshape(2, rows, parts * capacity)], axis=2)
        stencil = jnp.zeros_like(term)
        for apply_order in range(NBRS):
            stencil = stencil + weights[apply_order] * (
                jnp.take(extended, neighbours[apply_order], axis=2) - term
            )
        blocks = jnp.stack(
            [
                jnp.stack([intersection[0], -intersection[1]]),
                jnp.stack([intersection[1], intersection[0]]),
            ]
        )
        exchange = jnp.einsum("dmp,cdmj->cjp", full_frozen, blocks, precision=lax.Precision.HIGHEST)
        image = -0.5 * stencil + potential * term - exchange
        term = time_step / order * rotate(image)
        total = total + term
    return total


def solution(mesh):
    return jax.shard_map(
        body,
        mesh=mesh,
        in_specs=(
            P(None, "band", "mesh"),
            P(None, "band", "mesh"),
            P(None, "mesh"),
            P("mesh"),
            P("mesh", None, None),
            P(None, "mesh"),
        ),
        out_specs=P(None, "band", "mesh"),
        check_vma=False,
    )
```

profile of v0, /device:TPU:0, one launch (start us, length us, event | category | flops | bytes accessed | tf_op | source)
XLA Modules:
  0.0 581.9 jit_solution(13586005560089532101)
XLA Ops:
  2.1 14.4 %gather_fusion = f32[2048,2,16]{2,1,0:T(2,128)} fusion(f32[2,16,1024]{1,0,2:T(2,128)S(1)} %copy.119, s32[2048]{0:T(1024)S(1)} %fusion.108), kind=kCustom, calls=%fused_computation.clone | custom fusion | bytes 532480 | tf_op jit(solution)/shard_map/jit(_take)/gather | solution.py:29
  16.5 10.0 %broadcast_select_fusion.3 = f32[2048,2,16]{2,1,0:T(2,128)S(1)} fusion(f32[2048,2,16]{2,1,0:T(2,128)} %gather_fusion, pred[2048]{0:T(1024)(128)(4,1)S(1)} %compare_and_fusion), kind=kLoop, calls=%fused_computation.39 | loop fusion | flops 65536 | bytes 526336 | tf_op jit(solution)/shard_map/jit(_take)/select_n | solution.py:29
  39.6 14.2 %all_gather.3 = f32[2,32,1024]{2,1,0:T(8,128)S(1)} all-gather(f32[2,8,1024]{2,1,0:T(8,128)S(1)} %copy-done.34), channel_id=1, replica_groups=mesh['mesh'=8,'band'=4] {'band'}, dimensions={1}, use_global_device_ids=true | all-gather | bytes 327680 | tf_op jit(solution)/shard_map/all_gather | solution.py:20
  54.3 23.0 %psum.28 = f32[2,32,16]{1,2,0:T(8,128)S(1)} all-reduce(f32[2,32,16]{1,2,0:T(8,128)S(1)} %convolution_bitcast_fusion.7), channel_id=1, replica_groups=mesh['mesh'=8,'band'=4] {'mesh'}, use_global_device_ids=true, to_apply=%region_0.3 | all-reduce | flops 1024 | bytes 8192 | tf_op jit(solution)/shard_map/psum | solution.py:28
  84.0 7.6 %gather_fusion.1 = f32[1024,2,16]{2,1,0:T(2,128)} fusion(f32[2,16,3072]{1,0,2:T(2,128)S(1)} %copy.122, s32[1024]{0:T(1024)} %fusion.109), kind=kCustom, calls=%fused_computation.1.clone | custom fusion | bytes 266240 | tf_op jit(solution)/shard_map/jit(_take)/gather | solution.py:35
  93.7 7.6 %gather_fusion.2 = f32[1024,2,16]{2,1,0:T(2,128)} fusion(f32[2,16,3072]{1,0,2:T(2,128)S(1)} %copy.122, s32[1024]{0:T(1024)} %fusion.110), kind=kCustom, calls=%fused_computation.5.clone | custom fusion | bytes 266240 | tf_op jit(solution)/shard_map/jit(_take)/gather | solution.py:35
  103.3 7.6 %gather_fusion.3 = f32[1024,2,16]{2,1,0:T(2,128)} fusion(f32[2,16,3072]{1,0,2:T(2,128)S(1)} %copy.122, s32[1024]{0:T(1024)} %fusion.111), kind=kCustom, calls=%fused_computation.6.clone | custom fusion | bytes 266240 | tf_op jit(solution)/shard_map/jit(_take)/gather | solution.py:35
  112.9 7.6 %gather_fusion.4 = f32[1024,2,16]{2,1,0:T(2,128)} fusion(f32[2,16,3072]{1,0,2:T(2,128)S(1)} %copy.122, s32[1024]{0:T(1024)} %fusion.112), kind=kCustom, calls=%fused_computation.7.clone | custom fusion | bytes 266240 | tf_op jit(solution)/shard_map/jit(_take)/gather | solution.py:35
  122.5 7.6 %gather_fusion.5 = f32[1024,2,16]{2,1,0:T(2,128)} fusion(f32[2,16,3072]{1,0,2:T(2,128)S(1)} %copy.122, s32[1024]{0:T(1024)} %fusion.113), kind=kCustom, calls=%fused_computation.8.clone | custom fusion | bytes 266240 | tf_op jit(solution)/shard_map/jit(_take)/gather | solution.py:35
  132.1 7.6 %gather_fusion.6 = f32[1024,2,16]{2,1,0:T(2,128)} fusion(f32[2,16,3072]{1,0,2:T(2,128)S(1)} %copy.122, s32[1024]{0:T(1024)} %fusion.114), kind=kCustom, calls=%fused_computation.9.clone | custom fusion | bytes 266240 | tf_op jit(solution)/shard_map/jit(_take)/gather | solution.py:35
  141.7 7.5 %gather_fusion.7 = f32[1024,2,16]{2,1,0:T(2,128)} fusion(f32[2,16,3072]{1,0,2:T(2,128)S(1)} %copy.122, s32[1024]{0:T(1024)S(1)} %fusion.115), kind=kCustom, calls=%fused_computation.10.clone | custom fusion | bytes 266240 | tf_op jit(solution)/shard_map/jit(_take)/gather | solution.py:35
  151.2 7.5 %gather_fusion.8 = f32[1024,2,16]{2,1,0:T(2,128)} fusion(f32[2,16,3072]{1,0,2:T(2,128)S(1)} %copy.122, s32[1024]{0:T(1024)S(1)} %fusion.116), kind=kCustom, calls=%fused_computation.11.clone | custom fusion | bytes 266240 | tf_op jit(solution)/shard_map/jit(_take)/gather | solution.py:35
  163.5 22.3 %psum.29 = f32[2,32,16]{1,2,0:T(8,128)S(1)} all-reduce(f32[2,32,16]{1,2,0:T(8,128)S(1)} %convolution_bitcast_fusion.6), channel_id=1, replica_groups=mesh['mesh'=8,'band'=4] {'mesh'}, use_global_device_ids=true, to_apply=%region_1.4 | all-reduce | flops 1024 | bytes 8192 | tf_op jit(solution)/shard_map/psum | solution.py:28
  185.8 14.4 %gather_fusion.9 = f32[2048,2,16]{2,1,0:T(2,128)} fusion(f32[2,16,1024]{1,0,2:T(2,128)S(1)} %copy.138, s32[2048]{0:T(1024)S(1)} %fusion.108), kind=kCustom, calls=%fused_computation.2.clone | custom fusion | bytes 532480 | tf_op jit(solution)/shard_map/jit(_take)/gather | solution.py:29
  200.2 10.0 %broadcast_select_fusion.2 = f32[2048,2,16]{2,1,0:T(2,128)S(1)} fusion(f32[2048,2,16]{2,1,0:T(2,128)} %gather_fusion.9, pred[2048]{0:T(1024)(128)(4,1)S(1)} %copy-done.36), kind=kLoop, calls=%fused_computation.38 | loop fusion | flops 65536 | bytes 526336 | tf_op jit(solution)/shard_map/jit(_take)/select_n | solution.py:29
  216.3 6.1 %all-to-all-done.1 = f32[2,16,8,256]{3,1,0,2:T(8,128)S(1)} async-done(((f32[2,16,8,256]{3,1,0,2:T(8,128)}), f32[2,16,8,256]{3,1,0,2:T(8,128)S(1)}, u32[]{:S(2)}, u32[]{:S(2)}) %all-to-all-start.1) | async-done | bytes 262176 | tf_op jit(solution)/shard_map/all_to_all | solution.py:30
  227.3 7.6 %gather_fusion.10 = f32[1024,2,16]{2,1,0:T(2,128)} fusion(f32[2,16,3072]{1,0,2:T(2,128)S(1)} %copy.141, s32[1024]{0:T(1024)} %fusion.109), kind=kCustom, calls=%fused_computation.12.clone | custom fusion | bytes 266240 | tf_op jit(solution)/shard_map/jit(_take)/gather | solution.py:35
  235.0 7.6 %gather_fusion.11 = f32[1024,2,16]{2,1,0:T(2,128)} fusion(f32[2,16,3072]{1,0,2:T(2,128)S(1)} %copy.141, s32[1024]{0:T(1024)} %fusion.110), kind=kCustom, calls=%fused_computation.13.clone | custom fusion | bytes 266240 | tf_op jit(solution)/shard_map/jit(_take)/gather | solution.py:35
  242.6 7.6 %gather_fusion.12 = f32[1024,2,16]{2,1,0:T(2,128)} fusion(f32[2,16,3072]{1,0,2:T(2,128)S(1)} %copy.141, s32[1024]{0:T(1024)} %fusion.111), kind=kCustom, calls=%fused_computation.14.clone | custom fusion | bytes 266240 | tf_op jit(solution)/shard_map/jit(_take)/gather | solution.py:35
  250.2 7.6 %gather_fusion.13 = f32[1024,2,16]{2,1,0:T(2,128)} fusion(f32[2,16,3072]{1,0,2:T(2,128)S(1)} %copy.141, s32[1024]{0:T(1024)} %fusion.112), kind=kCustom, calls=%fused_computation.15.clone | custom fusion | bytes 266240 | tf_op jit(solution)/shard_map/jit(_take)/gather | solution.py:35
  257.8 7.6 %gather_fusion.14 = f32[1024,2,16]{2,1,0:T(2,128)} fusion(f32[2,16,3072]{1,0,2:T(2,128)S(1)} %copy.141, s32[1024]{0:T(1024)} %fusion.113), kind=kCustom, calls=%fused_computation.16.clone | custom fusion | bytes 266240 | tf_op jit(solution)/shard_map/jit(_take)/gather | solution.py:35
  265.4 7.6 %gather_fusion.15 = f32[1024,2,16]{2,1,0:T(2,128)} fusion(f32[2,16,3072]{1,0,2:T(2,128)S(1)} %copy.141, s32[1024]{0:T(1024)} %fusion.114), kind=kCustom, calls=%fused_computation.17.clone | custom fusion | bytes 266240 | tf_op jit(solution)/shard_map/jit(_take)/gather | solution.py:35
  273.0 7.5 %gather_fusion.16 = f32[1024,2,16]{2,1,0:T(2,128)} fusion(f32[2,16,3072]{1,0,2:T(2,128)S(1)} %copy.141, s32[1024]{0:T(1024)S(1)} %fusion.115), kind=kCustom, calls=%fused_computation.18.clone | custom fusion | bytes 266240 | tf_op jit(solution)/shard_map/jit(_take)/gather | solution.py:35
  280.5 7.5 %gather_fusion.17 = f32[1024,2,16]{2,1,0:T(2,128)} fusion(f32[2,16,3072]{1,0,2:T(2,128)S(1)} %copy.141, s32[1024]{0:T(1024)S(1)} %fusion.116), kind=kCustom, calls=%fused_computation.19.clone | custom fusion | bytes 266240 | tf_op jit(solution)/shard_map/jit(_take)/gather | solution.py:35
  303.7 22.3 %psum.30 = f32[2,32,16]{1,2,0:T(8,128)S(1)} all-reduce(f32[2,32,16]{1,2,0:T(8,128)S(1)} %convolution_bitcast_fusion.5), channel_id=1, replica_groups=mesh['mesh'=8,'band'=4] {'mesh'}, use_global_device_ids=true, to_apply=%region_2.5 | all-reduce | flops 1024 | bytes 8192 | tf_op jit(solution)/shard_map/psum | solution.py:28
  326.0 14.4 %gather_fusion.18 = f32[2048,2,16]{2,1,0:T(2,128)} fusion(f32[2,16,1024]{1,0,2:T(2,128)S(1)} %copy.157, s32[2048]{0:T(1024)S(1)} %fusion.108), kind=kCustom, calls=%fused_computation.3.clone | custom fusion | bytes 532480 | tf_op jit(solution)/shard_map/jit(_take)/gather | solution.py:29
  340.4 10.0 %broadcast_select_fusion.1 = f32[2048,2,16]{2,1,0:T(2,128)S(1)} fusion(f32[2048,2,16]{2,1,0:T(2,128)} %gather_fusion.18, pred[2048]{0:T(1024)(128)(4,1)S(1)} %copy-done.37), kind=kLoop, calls=%fused_computation.37 | loop fusion | flops 65536 | bytes 526336 | tf_op jit(solution)/shard_map/jit(_take)/select_n | solution.py:29
  356.3 6.2 %all-to-all-done.2 = f32[2,16,8,256]{3,1,0,2:T(8,128)S(1)} async-done(((f32[2,16,8,256]{3,1,0,2:T(8,128)}), f32[2,16,8,256]{3,1,0,2:T(8,128)S(1)}, u32[]{:S(2)}, u32[]{:S(2)}) %all-to-all-start.2) | async-done | bytes 262176 | tf_op jit(solution)/shard_map/all_to_all | solution.py:30
  367.5 7.6 %gather_fusion.19 = f32[1024,2,16]{2,1,0:T(2,128)} fusion(f32[2,16,3072]{1,0,2:T(2,128)S(1)} %copy.160, s32[1024]{0:T(1024)} %fusion.109), kind=kCustom, calls=%fused_computation.20.clone | custom fusion | bytes 266240 | tf_op jit(solution)/shard_map/jit(_take)/gather | solution.py:35
  375.2 7.6 %gather_fusion.20 = f32[1024,2,16]{2,1,0:T(2,128)} fusion(f32[2,16,3072]{1,0,2:T(2,128)S(1)} %copy.160, s32[1024]{0:T(1024)} %fusion.110), kind=kCustom, calls=%fused_computation.21.clone | custom fusion | bytes 266240 | tf_op jit(solution)/shard_map/jit(_take)/gather | solution.py:35
  382.8 7.6 %gather_fusion.21 = f32[1024,2,16]{2,1,0:T(2,128)} fusion(f32[2,16,3072]{1,0,2:T(2,128)S(1)} %copy.160, s32[1024]{0:T(1024)} %fusion.111), kind=kCustom, calls=%fused_computation.22.clone | custom fusion | bytes 266240 | tf_op jit(solution)/shard_map/jit(_take)/gather | solution.py:35
  390.4 7.6 %gather_fusion.22 = f32[1024,2,16]{2,1,0:T(2,128)} fusion(f32[2,16,3072]{1,0,2:T(2,128)S(1)} %copy.160, s32[1024]{0:T(1024)} %fusion.112), kind=kCustom, calls=%fused_computation.23.clone | custom fusion | bytes 266240 | tf_op jit(solution)/shard_map/jit(_take)/gather | solution.py:35
  398.0 7.6 %gather_fusion.23 = f32[1024,2,16]{2,1,0:T(2,128)} fusion(f32[2,16,3072]{1,0,2:T(2,128)S(1)} %copy.160, s32[1024]{0:T(1024)} %fusion.113), kind=kCustom, calls=%fused_computation.24.clone | custom fusion | bytes 266240 | tf_op jit(solution)/shard_map/jit(_take)/gather | solution.py:35
  405.6 7.6 %gather_fusion.24 = f32[1024,2,16]{2,1,0:T(2,128)} fusion(f32[2,16,3072]{1,0,2:T(2,128)S(1)} %copy.160, s32[1024]{0:T(1024)} %fusion.114), kind=kCustom, calls=%fused_computation.25.clone | custom fusion | bytes 266240 | tf_op jit(solution)/shard_map/jit(_take)/gather | solution.py:35
  413.2 7.5 %gather_fusion.25 = f32[1024,2,16]{2,1,0:T(2,128)} fusion(f32[2,16,3072]{1,0,2:T(2,128)S(1)} %copy.160, s32[1024]{0:T(1024)S(1)} %fusion.115), kind=kCustom, calls=%fused_computation.26.clone | custom fusion | bytes 266240 | tf_op jit(solution)/shard_map/jit(_take)/gather | solution.py:35
  420.7 7.5 %gather_fusion.26 = f32[1024,2,16]{2,1,0:T(2,128)} fusion(f32[2,16,3072]{1,0,2:T(2,128)S(1)} %copy.160, s32[1024]{0:T(1024)S(1)} %fusion.116), kind=kCustom, calls=%fused_computation.27.clone | custom fusion | bytes 266240 | tf_op jit(solution)/shard_map/jit(_take)/gather | solution.py:35
  443.8 22.3 %psum.31 = f32[2,32,16]{1,2,0:T(8,128)S(1)} all-reduce(f32[2,32,16]{1,2,0:T(8,128)S(1)} %convolution_bitcast_fusion.4), channel_id=1, replica_groups=mesh['mesh'=8,'band'=4] {'mesh'}, use_global_device_ids=true, to_apply=%region_3.6 | all-reduce | flops 1024 | bytes 8192 | tf_op jit(solution)/shard_map/psum | solution.py:28
  466.1 14.4 %gather_fusion.27 = f32[2048,2,16]{2,1,0:T(2,128)} fusion(f32[2,16,1024]{1,0,2:T(2,128)S(1)} %copy.176, s32[2048]{0:T(1024)S(1)} %fusion.108), kind=kCustom, calls=%fused_computation.4.clone | custom fusion | bytes 532480 | tf_op jit(solution)/shard_map/jit(_take)/gather | solution.py:29
  480.6 10.0 %broadcast_select_fusion = f32[2048,2,16]{2,1,0:T(2,128)S(1)} fusion(f32[2048,2,16]{2,1,0:T(2,128)} %gather_fusion.27, pred[2048]{0:T(1024)(128)(4,1)S(1)} %copy-done.38), kind=kLoop, calls=%fused_computation.36 | loop fusion | flops 65536 | bytes 526336 | tf_op jit(solution)/shard_map/jit(_take)/select_n | solution.py:29
  496.8 6.0 %all-to-all-done.3 = f32[2,16,8,256]{3,1,0,2:T(8,128)S(1)} async-done(((f32[2,16,8,256]{3,1,0,2:T(8,128)}), f32[2,16,8,256]{3,1,0,2:T(8,128)S(1)}, u32[]{:S(2)}, u32[]{:S(2)}) %all-to-all-start.3) | async-done | bytes 262176 | tf_op jit(solution)/shard_map/all_to_all | solution.py:30
  507.8 7.6 %gather_fusion.28 = f32[1024,2,16]{2,1,0:T(2,128)} fusion(f32[2,16,3072]{1,0,2:T(2,128)S(1)} %copy.179, s32[1024]{0:T(1024)} %fusion.109), kind=kCustom, calls=%fused_computation.28.clone | custom fusion | bytes 266240 | tf_op jit(solution)/shard_map/jit(_take)/gather | solution.py:35
  515.4 7.6 %gather_fusion.29 = f32[1024,2,16]{2,1,0:T(2,128)} fusion(f32[2,16,3072]{1,0,2:T(2,128)S(1)} %copy.179, s32[1024]{0:T(1024)} %fusion.110), kind=kCustom, calls=%fused_computation.29.clone | custom fusion | bytes 266240 | tf_op jit(solution)/shard_map/jit(_take)/gather | solution.py:35
  523.0 7.6 %gather_fusion.30 = f32[1024,2,16]{2,1,0:T(2,128)} fusion(f32[2,16,3072]{1,0,2:T(2,128)S(1)} %copy.179, s32[1024]{0:T(1024)} %fusion.111), kind=kCustom, calls=%fused_computation.30.clone | custom fusion | bytes 266240 | tf_op jit(solution)/shard_map/jit(_take)/gather | solution.py:35
  530.6 7.6 %gather_fusion.31 = f32[1024,2,16]{2,1,0:T(2,128)} fusion(f32[2,16,3072]{1,0,2:T(2,128)S(1)} %copy.179, s32[1024]{0:T(1024)} %fusion.112), kind=kCustom, calls=%fused_computation.31.clone | custom fusion | bytes 266240 | tf_op jit(solution)/shard_map/jit(_take)/gather | solution.py:35
  538.2 7.5 %gather_fusion.32 = f32[1024,2,16]{2,1,0:T(2,128)} fusion(f32[2,16,3072]{1,0,2:T(2,128)S(1)} %copy.179, s32[1024]{0:T(1024)S(1)} %copy-done.29), kind=kCustom, calls=%fused_computation.32.clone | custom fusion | bytes 266240 | tf_op jit(solution)/shard_map/jit(_take)/gather | solution.py:35
  545.7 7.5 %gather_fusion.33 = f32[1024,2,16]{2,1,0:T(2,128)} fusion(f32[2,16,3072]{1,0,2:T(2,128)S(1)} %copy.179, s32[1024]{0:T(1024)S(1)} %copy-done.28), kind=kCustom, calls=%fused_computation.33.clone | custom fusion | bytes 266240 | tf_op jit(solution)/shard_map/jit(_take)/gather | solution.py:35
  553.2 7.5 %gather_fusion.34 = f32[1024,2,16]{2,1,0:T(2,128)} fusion(f32[2,16,3072]{1,0,2:T(2,128)S(1)} %copy.179, s32[1024]{0:T(1024)S(1)} %fusion.115), kind=kCustom, calls=%fused_computation.34.clone | custom fusion | bytes 266240 | tf_op jit(solution)/shard_map/jit(_take)/gather | solution.py:35
  560.7 7.5 %gather_fusion.35 = f32[1024,2,16]{2,1,0:T(2,128)} fusion(f32[2,16,3072]{1,0,2:T(2,128)S(1)} %copy.179, s32[1024]{0:T(1024)S(1)} %fusion.116), kind=kCustom, calls=%fused_computation.35.clone | custom fusion | bytes 266240 | tf_op jit(solution)/shard_map/jit(_take)/gather | solution.py:35
  (194 shorter events, 118.8 us)
Async XLA Ops:
  0.7 27.7 %copy-start.35 = (pred[2048]{0:T(1024)(128)(4,1)}, pred[2048]{0:T(1024)(128)(4,1)S(1)}, u32[]{:S(2)}) copy-start(pred[2048]{0:T(1024)(128)(4,1)S(1)} %compare_and_fusion) | copy-start | bytes 6148
  16.5 17.1 %copy-start = (f32[2,16,1024]{2,1,0:T(8,128)S(1)}, f32[2,16,1024]{2,1,0:T(8,128)}, u32[]{:S(2)}) copy-start(f32[2,16,1024]{2,1,0:T(8,128)} %param.10) | copy-start | bytes 393220
  16.5 17.1 %copy-start.39 = (s32[8,1024]{1,0:T(8,128)S(1)}, s32[8,1024]{1,0:T(8,128)}, u32[]{:S(2)}) copy-start(s32[8,1024]{1,0:T(8,128)} %param.15) | copy-start | bytes 98308
  16.5 23.1 %copy-start.34 = (f32[2,8,1024]{2,1,0:T(8,128)S(1)}, f32[2,8,1024]{2,1,0:T(8,128)}, u32[]{:S(2)}) copy-start(f32[2,8,1024]{2,1,0:T(8,128)} %param.11) | copy-start | bytes 196612
  26.5 50.7 %copy-start.41 = (f32[1024]{0:T(1024)S(1)}, f32[1024]{0:T(1024)}, u32[]{:S(2)}) copy-start(f32[1024]{0:T(1024)} %param.13) | copy-start | bytes 12292
  26.6 51.9 %copy-start.40 = (f32[8,1024]{1,0:T(8,128)S(1)}, f32[8,1024]{1,0:T(8,128)}, u32[]{:S(2)}) copy-start(f32[8,1024]{1,0:T(8,128)} %param.12) | copy-start | bytes 98308
  28.5 50.6 %all-to-all-start = ((f32[2,16,8,256]{3,1,0,2:T(8,128)}), f32[2,16,8,256]{3,1,0,2:T(8,128)S(1)}, u32[]{:S(2)}, u32[]{:S(2)}) async-start(f32[2,16,8,256]{3,1,0,2:T(8,128)} %copy.120), calls=%async_computation | async-start | bytes 524288 | tf_op jit(solution)/shard_map/all_to_all | solution.py:30
  158.7 41.6 %copy-start.36 = (pred[2048]{0:T(1024)(128)(4,1)S(1)}, pred[2048]{0:T(1024)(128)(4,1)}, u32[]{:S(2)}) copy-start(pred[2048]{0:T(1024)(128)(4,1)} %copy-done.35) | copy-start | bytes 6148
  161.9 0.6 copy-start.11
  161.9 0.6 copy-start.13
  212.1 10.3 %all-to-all-start.1 = ((f32[2,16,8,256]{3,1,0,2:T(8,128)}), f32[2,16,8,256]{3,1,0,2:T(8,128)S(1)}, u32[]{:S(2)}, u32[]{:S(2)}) async-start(f32[2,16,8,256]{3,1,0,2:T(8,128)} %copy.139), calls=%async_computation.1 | async-start | bytes 524288 | tf_op jit(solution)/shard_map/all_to_all | solution.py:30
  287.9 10.4 %copy-start.9 = (f32[1024,2,16]{2,1,0:T(2,128)S(1)}, f32[1024,2,16]{2,1,0:T(2,128)}, u32[]{:S(2)}) copy-start(f32[1024,2,16]{2,1,0:T(2,128)} %gather_fusion.15) | copy-start | bytes 393220
  290.0 9.3 %copy-start.7 = (f32[1024,2,16]{2,1,0:T(2,128)S(1)}, f32[1024,2,16]{2,1,0:T(2,128)}, u32[]{:S(2)}) copy-start(f32[1024,2,16]{2,1,0:T(2,128)} %gather_fusion.16) | copy-start | bytes 393220
  292.2 7.6 %copy-start.5 = (f32[1024,2,16]{2,1,0:T(2,128)S(1)}, f32[1024,2,16]{2,1,0:T(2,128)}, u32[]{:S(2)}) copy-start(f32[1024,2,16]{2,1,0:T(2,128)} %gather_fusion.17) | copy-start | bytes 393220
  299.8 40.6 %copy-start.37 = (pred[2048]{0:T(1024)(128)(4,1)S(1)}, pred[2048]{0:T(1024)(128)(4,1)}, u32[]{:S(2)}) copy-start(pred[2048]{0:T(1024)(128)(4,1)} %copy-done.35) | copy-start | bytes 6148
  302.1 0.6 copy-start.15
  302.1 0.6 copy-start.17
  352.3 10.3 %all-to-all-start.2 = ((f32[2,16,8,256]{3,1,0,2:T(8,128)}), f32[2,16,8,256]{3,1,0,2:T(8,128)S(1)}, u32[]{:S(2)}, u32[]{:S(2)}) async-start(f32[2,16,8,256]{3,1,0,2:T(8,128)} %copy.158), calls=%async_computation.2 | async-start | bytes 524288 | tf_op jit(solution)/shard_map/all_to_all | solution.py:30
  428.1 10.4 %copy-start.10 = (f32[1024,2,16]{2,1,0:T(2,128)S(1)}, f32[1024,2,16]{2,1,0:T(2,128)}, u32[]{:S(2)}) copy-start(f32[1024,2,16]{2,1,0:T(2,128)} %gather_fusion.24) | copy-start | bytes 393220
  430.2 9.3 %copy-start.8 = (f32[1024,2,16]{2,1,0:T(2,128)S(1)}, f32[1024,2,16]{2,1,0:T(2,128)}, u32[]{:S(2)}) copy-start(f32[1024,2,16]{2,1,0:T(2,128)} %gather_fusion.25) | copy-start | bytes 393220
  432.4 7.6 %copy-start.6 = (f32[1024,2,16]{2,1,0:T(2,128)S(1)}, f32[1024,2,16]{2,1,0:T(2,128)}, u32[]{:S(2)}) copy-start(f32[1024,2,16]{2,1,0:T(2,128)} %gather_fusion.26) | copy-start | bytes 393220
  440.0 40.6 %copy-start.38 = (pred[2048]{0:T(1024)(128)(4,1)S(1)}, pred[2048]{0:T(1024)(128)(4,1)}, u32[]{:S(2)}) copy-start(pred[2048]{0:T(1024)(128)(4,1)} %copy-done.35) | copy-start | bytes 6148
  442.2 0.6 copy-start.19
  442.2 0.6 copy-start.21
  492.4 45.7 %copy-start.29 = (s32[1024]{0:T(1024)S(1)}, s32[1024]{0:T(1024)}, u32[]{:S(2)}) copy-start(s32[1024]{0:T(1024)} %fusion.113) | copy-start | bytes 12292
  492.4 10.4 %all-to-all-start.3 = ((f32[2,16,8,256]{3,1,0,2:T(8,128)}), f32[2,16,8,256]{3,1,0,2:T(8,128)S(1)}, u32[]{:S(2)}, u32[]{:S(2)}) async-start(f32[2,16,8,256]{3,1,0,2:T(8,128)} %copy.177), calls=%async_computation.3 | async-start | bytes 524288 | tf_op jit(solution)/shard_map/all_to_all | solution.py:30
  496.2 49.5 %copy-start.28 = (s32[1024]{0:T(1024)S(1)}, s32[1024]{0:T(1024)}, u32[]{:S(2)}) copy-start(s32[1024]{0:T(1024)} %fusion.114) | copy-start | bytes 12292
  568.2 6.2 %copy-start.1 = (f32[1024,2,16]{2,1,0:T(2,128)S(1)}, f32[1024,2,16]{2,1,0:T(2,128)}, u32[]{:S(2)}) copy-start(f32[1024,2,16]{2,1,0:T(2,128)} %gather_fusion.31) | copy-start | bytes 393220
  568.2 7.3 %copy-start.2 = (f32[1024,2,16]{2,1,0:T(2,128)S(1)}, f32[1024,2,16]{2,1,0:T(2,128)}, u32[]{:S(2)}) copy-start(f32[1024,2,16]{2,1,0:T(2,128)} %gather_fusion.32) | copy-start | bytes 393220
  568.2 8.4 %copy-start.3 = (f32[1024,2,16]{2,1,0:T(2,128)S(1)}, f32[1024,2,16]{2,1,0:T(2,128)}, u32[]{:S(2)}) copy-start(f32[1024,2,16]{2,1,0:T(2,128)} %gather_fusion.33) | copy-start | bytes 393220
  574.4 5.2 copy-start.30
  574.4 5.2 copy-start.31
  574.4 5.2 copy-start.32
  574.4 5.2 copy-start.33
  575.5 3.6 copy-start.4
  576.6 3.0 copy-start.20
  576.6 3.0 copy-start.22
  576.6 3.0 copy-start.23
  576.6 3.0 copy-start.24
  576.6 3.0 copy-start.25
  576.6 3.0 copy-start.26
  576.6 3.0 copy-start.27
  576.6 4.5 copy-start.12
  576.7 4.5 copy-start.14
  576.7 4.5 copy-start.16
  576.7 4.5 copy-start.18
where the time goes:
time: 585 us; the launch traced here: 582 us
  local copies, waits for them, and re-layouts  382 us (65%)
  blocking collectives  104 us (18%)
  other arithmetic  53 us (9%)
  waiting for transfers between devices  18.3 us (3%)
  starting transfers between devices  15.9 us (3%)
  matrix products  8.07 us (1%)
    gather x64, local copies, waits for them, and re-layouts, body(): jnp.take(extended, neighbours[apply_order], axis=2) - term  293 us
    psum x4, blocking collectives, body(): intersection = lax.psum(partial_intersection, 'mesh')  89.9 us
    gather x4, local copies, waits for them, and re-layouts, body(): jnp.take(term, routes.reshape(-1), axis=2).reshape(2, rows, parts, capacity)  57.7 us
    select_n x4, other arithmetic, body(): jnp.take(term, routes.reshape(-1), axis=2).reshape(2, rows, parts, capacity)  39.9 us
    all_to_all x4, waiting for transfers between devices, body(): lax.all_to_all(packed, 'mesh', split_axis=2, concat_axis=2, tiled=True)  18.3 us
    concatenate x4, local copies, waits for them, and re-layouts, body(): jnp.concatenate([term, arrived.reshape(2, rows, parts * capacity)], axis=2)  16.6 us
    all_to_all x4, starting transfers between devices, body(): lax.all_to_all(packed, 'mesh', split_axis=2, concat_axis=2, tiled=True)  15.9 us
    all_gather x1, blocking collectives, body(): full_frozen = lax.all_gather(frozen, 'band', axis=1, tiled=True)  14.2 us
  transfers between devices with their start and end apart: 4, of which 3 were waited for; matrix products, arithmetic and copies ran while one was open for 2% of the time, Pallas kernels for 0%

commit v1 on v0

--- a/solution.py
+++ b/solution.py
@@ -25,7 +25,7 @@
         partial_intersection = jnp.einsum(
             "cmp,ocjp->omj", full_frozen, paired, precision=lax.Precision.HIGHEST
         )
-        intersection = lax.psum(partial_intersection, "mesh")
+        intersection = jnp.sum(lax.all_gather(partial_intersection, "mesh"), axis=0)
         packed = jnp.take(term, routes.reshape(-1), axis=2).reshape(2, rows, parts, capacity)
         arrived = lax.all_to_all(packed, "mesh", split_axis=2, concat_axis=2, tiled=True)
         extended = jnp.concatenate([term, arrived.reshape(2, rows, parts * capacity)], axis=2)

time: 585 us -> 530 us (0.906)
  blocking collectives: 104 us -> 49.4 us
    psum x4 -> x0, blocking collectives: 89.9 us -> none  [body(): intersection = lax.psum(partial_intersection, 'mesh')]
    all_gather x0 -> x4, blocking collectives: none -> 35.2 us  [body(): intersection = jnp.sum(lax.all_gather(partial_intersection, 'mesh'), axis=0)]
where the time goes in v1:
time: 530 us; the launch traced here: 527 us
  local copies, waits for them, and re-layouts  382 us (72%)
  other arithmetic  53 us (10%)
  blocking collectives  49.4 us (9%)
  waiting for transfers between devices  18.3 us (3%)
  starting transfers between devices  15.9 us (3%)
  matrix products  8.06 us (2%)
    gather x64, local copies, waits for them, and re-layouts, body(): jnp.take(extended, neighbours[apply_order], axis=2) - term  293 us
    gather x4, local copies, waits for them, and re-layouts, body(): jnp.take(term, routes.reshape(-1), axis=2).reshape(2, rows, parts, capacity)  57.7 us
    select_n x4, other arithmetic, body(): jnp.take(term, routes.reshape(-1), axis=2).reshape(2, rows, parts, capacity)  39.9 us
    all_gather x4, blocking collectives, body(): intersection = jnp.sum(lax.all_gather(partial_intersection, 'mesh'), axis=0)  35.2 us
    all_to_all x4, waiting for transfers between devices, body(): lax.all_to_all(packed, 'mesh', split_axis=2, concat_axis=2, tiled=True)  18.3 us
    concatenate x4, local copies, waits for them, and re-layouts, body(): jnp.concatenate([term, arrived.reshape(2, rows, parts * capacity)], axis=2)  16.6 us
    all_to_all x4, starting transfers between devices, body(): lax.all_to_all(packed, 'mesh', split_axis=2, concat_axis=2, tiled=True)  15.9 us
    all_gather x1, blocking collectives, body(): full_frozen = lax.all_gather(frozen, 'band', axis=1, tiled=True)  14.2 us
  transfers between devices with their start and end apart: 4, of which 3 were waited for; matrix products, arithmetic and copies ran while one was open for 2% of the time, Pallas kernels for 0%

profile of v1, /device:TPU:0, one launch (start us, length us, event | category | flops | bytes accessed | tf_op | source)
XLA Modules:
  0.0 527.3 jit_solution(10465270733937517783)
XLA Ops:
  2.1 14.4 %gather_fusion = f32[2048,2,16]{2,1,0:T(2,128)} fusion(f32[2,16,1024]{1,0,2:T(2,128)S(1)} %copy.119, s32[2048]{0:T(1024)S(1)} %fusion.108), kind=kCustom, calls=%fused_computation.clone | custom fusion | bytes 532480 | tf_op jit(solution)/shard_map/jit(_take)/gather | solution.py:29
  16.5 10.0 %broadcast_select_fusion.3 = f32[2048,2,16]{2,1,0:T(2,128)S(1)} fusion(f32[2048,2,16]{2,1,0:T(2,128)} %gather_fusion, pred[2048]{0:T(1024)(128)(4,1)S(1)} %compare_and_fusion), kind=kLoop, calls=%fused_computation.39 | loop fusion | flops 65536 | bytes 526336 | tf_op jit(solution)/shard_map/jit(_take)/select_n | solution.py:29
  39.6 14.2 %all_gather.27 = f32[2,32,1024]{2,1,0:T(8,128)S(1)} all-gather(f32[2,8,1024]{2,1,0:T(8,128)S(1)} %copy-done.34), channel_id=1, replica_groups=mesh['mesh'=8,'band'=4] {'band'}, dimensions={1}, use_global_device_ids=true | all-gather | bytes 327680 | tf_op jit(solution)/shard_map/all_gather | solution.py:20
  54.3 9.5 %all-gather = f32[16,32,16]{1,2,0:T(8,128)S(1)} all-gather(f32[2,32,16]{1,2,0:T(8,128)S(1)} %convolution_bitcast_fusion.7), channel_id=2, replica_groups=mesh['mesh'=8,'band'=4] {'mesh'}, dimensions={0}, use_global_device_ids=true | all-gather | bytes 36864 | tf_op jit(solution)/shard_map/all_gather | solution.py:28
  70.6 7.6 %gather_fusion.1 = f32[1024,2,16]{2,1,0:T(2,128)} fusion(f32[2,16,3072]{1,0,2:T(2,128)S(1)} %copy.122, s32[1024]{0:T(1024)} %fusion.109), kind=kCustom, calls=%fused_computation.1.clone | custom fusion | bytes 266240 | tf_op jit(solution)/shard_map/jit(_take)/gather | solution.py:35
  80.2 7.6 %gather_fusion.2 = f32[1024,2,16]{2,1,0:T(2,128)} fusion(f32[2,16,3072]{1,0,2:T(2,128)S(1)} %copy.122, s32[1024]{0:T(1024)} %fusion.110), kind=kCustom, calls=%fused_computation.5.clone | custom fusion | bytes 266240 | tf_op jit(solution)/shard_map/jit(_take)/gather | solution.py:35
  89.8 7.6 %gather_fusion.3 = f32[1024,2,16]{2,1,0:T(2,128)} fusion(f32[2,16,3072]{1,0,2:T(2,128)S(1)} %copy.122, s32[1024]{0:T(1024)} %fusion.111), kind=kCustom, calls=%fused_computation.6.clone | custom fusion | bytes 266240 | tf_op jit(solution)/shard_map/jit(_take)/gather | solution.py:35
  99.4 7.6 %gather_fusion.4 = f32[1024,2,16]{2,1,0:T(2,128)} fusion(f32[2,16,3072]{1,0,2:T(2,128)S(1)} %copy.122, s32[1024]{0:T(1024)} %fusion.112), kind=kCustom, calls=%fused_computation.7.clone | custom fusion | bytes 266240 | tf_op jit(solution)/shard_map/jit(_take)/gather | solution.py:35
  109.1 7.6 %gather_fusion.5 = f32[1024,2,16]{2,1,0:T(2,128)} fusion(f32[2,16,3072]{1,0,2:T(2,128)S(1)} %copy.122, s32[1024]{0:T(1024)} %fusion.113), kind=kCustom, calls=%fused_computation.8.clone | custom fusion | bytes 266240 | tf_op jit(solution)/shard_map/jit(_take)/gather | solution.py:35
  118.7 7.6 %gather_fusion.6 = f32[1024,2,16]{2,1,0:T(2,128)} fusion(f32[2,16,3072]{1,0,2:T(2,128)S(1)} %copy.122, s32[1024]{0:T(1024)} %fusion.114), kind=kCustom, calls=%fused_computation.9.clone | custom fusion | bytes 266240 | tf_op jit(solution)/shard_map/jit(_take)/gather | solution.py:35
  128.3 7.5 %gather_fusion.7 = f32[1024,2,16]{2,1,0:T(2,128)} fusion(f32[2,16,3072]{1,0,2:T(2,128)S(1)} %copy.122, s32[1024]{0:T(1024)S(1)} %fusion.115), kind=kCustom, calls=%fused_computation.10.clone | custom fusion | bytes 266240 | tf_op jit(solution)/shard_map/jit(_take)/gather | solution.py:35
  137.8 7.5 %gather_fusion.8 = f32[1024,2,16]{2,1,0:T(2,128)} fusion(f32[2,16,3072]{1,0,2:T(2,128)S(1)} %copy.122, s32[1024]{0:T(1024)S(1)} %fusion.116), kind=kCustom, calls=%fused_computation.11.clone | custom fusion | bytes 266240 | tf_op jit(solution)/shard_map/jit(_take)/gather | solution.py:35
  150.0 9.2 %all-gather.1 = f32[16,32,16]{1,2,0:T(8,128)S(1)} all-gather(f32[2,32,16]{1,2,0:T(8,128)S(1)} %convolution_bitcast_fusion.6), channel_id=3, replica_groups=mesh['mesh'=8,'band'=4] {'mesh'}, dimensions={0}, use_global_device_ids=true | all-gather | bytes 36864 | tf_op jit(solution)/shard_map/all_gather | solution.py:28
  159.3 14.4 %gather_fusion.9 = f32[2048,2,16]{2,1,0:T(2,128)} fusion(f32[2,16,1024]{1,0,2:T(2,128)S(1)} %copy.138, s32[2048]{0:T(1024)S(1)} %fusion.108), kind=kCustom, calls=%fused_computation.2.clone | custom fusion | bytes 532480 | tf_op jit(solution)/shard_map/jit(_take)/gather | solution.py:29
  173.7 10.0 %broadcast_select_fusion.2 = f32[2048,2,16]{2,1,0:T(2,128)S(1)} fusion(f32[2048,2,16]{2,1,0:T(2,128)} %gather_fusion.9, pred[2048]{0:T(1024)(128)(4,1)S(1)} %copy-done.36), kind=kLoop, calls=%fused_computation.38 | loop fusion | flops 65536 | bytes 526336 | tf_op jit(solution)/shard_map/jit(_take)/select_n | solution.py:29
  189.8 6.1 %all-to-all-done.1 = f32[2,16,8,256]{3,1,0,2:T(8,128)S(1)} async-done(((f32[2,16,8,256]{3,1,0,2:T(8,128)}), f32[2,16,8,256]{3,1,0,2:T(8,128)S(1)}, u32[]{:S(2)}, u32[]{:S(2)}) %all-to-all-start.1) | async-done | bytes 262176 | tf_op jit(solution)/shard_map/all_to_all | solution.py:30
  200.8 7.6 %gather_fusion.10 = f32[1024,2,16]{2,1,0:T(2,128)} fusion(f32[2,16,3072]{1,0,2:T(2,128)S(1)} %copy.141, s32[1024]{0:T(1024)} %fusion.109), kind=kCustom, calls=%fused_computation.12.clone | custom fusion | bytes 266240 | tf_op jit(solution)/shard_map/jit(_take)/gather | solution.py:35
  208.4 7.6 %gather_fusion.11 = f32[1024,2,16]{2,1,0:T(2,128)} fusion(f32[2,16,3072]{1,0,2:T(2,128)S(1)} %copy.141, s32[1024]{0:T(1024)} %fusion.110), kind=kCustom, calls=%fused_computation.13.clone | custom fusion | bytes 266240 | tf_op jit(solution)/shard_map/jit(_take)/gather | solution.py:35
  216.0 7.6 %gather_fusion.12 = f32[1024,2,16]{2,1,0:T(2,128)} fusion(f32[2,16,3072]{1,0,2:T(2,128)S(1)} %copy.141, s32[1024]{0:T(1024)} %fusion.111), kind=kCustom, calls=%fused_computation.14.clone | custom fusion | bytes 266240 | tf_op jit(solution)/shard_map/jit(_take)/gather | solution.py:35
  223.6 7.6 %gather_fusion.13 = f32[1024,2,16]{2,1,0:T(2,128)} fusion(f32[2,16,3072]{1,0,2:T(2,128)S(1)} %copy.141, s32[1024]{0:T(1024)} %fusion.112), kind=kCustom, calls=%fused_computation.15.clone | custom fusion | bytes 266240 | tf_op jit(solution)/shard_map/jit(_take)/gather | solution.py:35
  231.3 7.6 %gather_fusion.14 = f32[1024,2,16]{2,1,0:T(2,128)} fusion(f32[2,16,3072]{1,0,2:T(2,128)S(1)} %copy.141, s32[1024]{0:T(1024)} %fusion.113), kind=kCustom, calls=%fused_computation.16.clone | custom fusion | bytes 266240 | tf_op jit(solution)/shard_map/jit(_take)/gather | solution.py:35
  238.9 7.6 %gather_fusion.15 = f32[1024,2,16]{2,1,0:T(2,128)} fusion(f32[2,16,3072]{1,0,2:T(2,128)S(1)} %copy.141, s32[1024]{0:T(1024)} %fusion.114), kind=kCustom, calls=%fused_computation.17.clone | custom fusion | bytes 266240 | tf_op jit(solution)/shard_map/jit(_take)/gather | solution.py:35
  246.5 7.5 %gather_fusion.16 = f32[1024,2,16]{2,1,0:T(2,128)} fusion(f32[2,16,3072]{1,0,2:T(2,128)S(1)} %copy.141, s32[1024]{0:T(1024)S(1)} %fusion.115), kind=kCustom, calls=%fused_computation.18.clone | custom fusion | bytes 266240 | tf_op jit(solution)/shard_map/jit(_take)/gather | solution.py:35
  253.9 7.5 %gather_fusion.17 = f32[1024,2,16]{2,1,0:T(2,128)} fusion(f32[2,16,3072]{1,0,2:T(2,128)S(1)} %copy.141, s32[1024]{0:T(1024)S(1)} %fusion.116), kind=kCustom, calls=%fused_computation.19.clone | custom fusion | bytes 266240 | tf_op jit(solution)/shard_map/jit(_take)/gather | solution.py:35
  277.1 8.3 %all-gather.2 = f32[16,32,16]{1,2,0:T(8,128)S(1)} all-gather(f32[2,32,16]{1,2,0:T(8,128)S(1)} %convolution_bitcast_fusion.5), channel_id=4, replica_groups=mesh['mesh'=8,'band'=4] {'mesh'}, dimensions={0}, use_global_device_ids=true | all-gather | bytes 36864 | tf_op jit(solution)/shard_map/all_gather | solution.py:28
  285.4 14.4 %gather_fusion.18 = f32[2048,2,16]{2,1,0:T(2,128)} fusion(f32[2,16,1024]{1,0,2:T(2,128)S(1)} %copy.157, s32[2048]{0:T(1024)S(1)} %fusion.108), kind=kCustom, calls=%fused_computation.3.clone | custom fusion | bytes 532480 | tf_op jit(solution)/shard_map/jit(_take)/gather | solution.py:29
  299.8 10.0 %broadcast_select_fusion.1 = f32[2048,2,16]{2,1,0:T(2,128)S(1)} fusion(f32[2048,2,16]{2,1,0:T(2,128)} %gather_fusion.18, pred[2048]{0:T(1024)(128)(4,1)S(1)} %copy-done.37), kind=kLoop, calls=%fused_computation.37 | loop fusion | flops 65536 | bytes 526336 | tf_op jit(solution)/shard_map/jit(_take)/select_n | solution.py:29
  315.7 6.2 %all-to-all-done.2 = f32[2,16,8,256]{3,1,0,2:T(8,128)S(1)} async-done(((f32[2,16,8,256]{3,1,0,2:T(8,128)}), f32[2,16,8,256]{3,1,0,2:T(8,128)S(1)}, u32[]{:S(2)}, u32[]{:S(2)}) %all-to-all-start.2) | async-done | bytes 262176 | tf_op jit(solution)/shard_map/all_to_all | solution.py:30
  326.9 7.6 %gather_fusion.19 = f32[1024,2,16]{2,1,0:T(2,128)} fusion(f32[2,16,3072]{1,0,2:T(2,128)S(1)} %copy.160, s32[1024]{0:T(1024)} %fusion.109), kind=kCustom, calls=%fused_computation.20.clone | custom fusion | bytes 266240 | tf_op jit(solution)/shard_map/jit(_take)/gather | solution.py:35
  334.6 7.6 %gather_fusion.20 = f32[1024,2,16]{2,1,0:T(2,128)} fusion(f32[2,16,3072]{1,0,2:T(2,128)S(1)} %copy.160, s32[1024]{0:T(1024)} %fusion.110), kind=kCustom, calls=%fused_computation.21.clone | custom fusion | bytes 266240 | tf_op jit(solution)/shard_map/jit(_take)/gather | solution.py:35
  342.2 7.6 %gather_fusion.21 = f32[1024,2,16]{2,1,0:T(2,128)} fusion(f32[2,16,3072]{1,0,2:T(2,128)S(1)} %copy.160, s32[1024]{0:T(1024)} %fusion.111), kind=kCustom, calls=%fused_computation.22.clone | custom fusion | bytes 266240 | tf_op jit(solution)/shard_map/jit(_take)/gather | solution.py:35
  349.8 7.6 %gather_fusion.22 = f32[1024,2,16]{2,1,0:T(2,128)} fusion(f32[2,16,3072]{1,0,2:T(2,128)S(1)} %copy.160, s32[1024]{0:T(1024)} %fusion.112), kind=kCustom, calls=%fused_computation.23.clone | custom fusion | bytes 266240 | tf_op jit(solution)/shard_map/jit(_take)/gather | solution.py:35
  357.4 7.6 %gather_fusion.23 = f32[1024,2,16]{2,1,0:T(2,128)} fusion(f32[2,16,3072]{1,0,2:T(2,128)S(1)} %copy.160, s32[1024]{0:T(1024)} %fusion.113), kind=kCustom, calls=%fused_computation.24.clone | custom fusion | bytes 266240 | tf_op jit(solution)/shard_map/jit(_take)/gather | solution.py:35
  365.0 7.6 %gather_fusion.24 = f32[1024,2,16]{2,1,0:T(2,128)} fusion(f32[2,16,3072]{1,0,2:T(2,128)S(1)} %copy.160, s32[1024]{0:T(1024)} %fusion.114), kind=kCustom, calls=%fused_computation.25.clone | custom fusion | bytes 266240 | tf_op jit(solution)/shard_map/jit(_take)/gather | solution.py:35
  372.6 7.5 %gather_fusion.25 = f32[1024,2,16]{2,1,0:T(2,128)} fusion(f32[2,16,3072]{1,0,2:T(2,128)S(1)} %copy.160, s32[1024]{0:T(1024)S(1)} %fusion.115), kind=kCustom, calls=%fused_computation.26.clone | custom fusion | bytes 266240 | tf_op jit(solution)/shard_map/jit(_take)/gather | solution.py:35
  380.1 7.5 %gather_fusion.26 = f32[1024,2,16]{2,1,0:T(2,128)} fusion(f32[2,16,3072]{1,0,2:T(2,128)S(1)} %copy.160, s32[1024]{0:T(1024)S(1)} %fusion.116), kind=kCustom, calls=%fused_computation.27.clone | custom fusion | bytes 266240 | tf_op jit(solution)/shard_map/jit(_take)/gather | solution.py:35
  403.3 8.3 %all-gather.3 = f32[16,32,16]{1,2,0:T(8,128)S(1)} all-gather(f32[2,32,16]{1,2,0:T(8,128)S(1)} %convolution_bitcast_fusion.4), channel_id=5, replica_groups=mesh['mesh'=8,'band'=4] {'mesh'}, dimensions={0}, use_global_device_ids=true | all-gather | bytes 36864 | tf_op jit(solution)/shard_map/all_gather | solution.py:28
  411.5 14.4 %gather_fusion.27 = f32[2048,2,16]{2,1,0:T(2,128)} fusion(f32[2,16,1024]{1,0,2:T(2,128)S(1)} %copy.176, s32[2048]{0:T(1024)S(1)} %fusion.108), kind=kCustom, calls=%fused_computation.4.clone | custom fusion | bytes 532480 | tf_op jit(solution)/shard_map/jit(_take)/gather | solution.py:29
  426.0 10.0 %broadcast_select_fusion = f32[2048,2,16]{2,1,0:T(2,128)S(1)} fusion(f32[2048,2,16]{2,1,0:T(2,128)} %gather_fusion.27, pred[2048]{0:T(1024)(128)(4,1)S(1)} %copy-done.38), kind=kLoop, calls=%fused_computation.36 | loop fusion | flops 65536 | bytes 526336 | tf_op jit(solution)/shard_map/jit(_take)/select_n | solution.py:29
  442.2 6.0 %all-to-all-done.3 = f32[2,16,8,256]{3,1,0,2:T(8,128)S(1)} async-done(((f32[2,16,8,256]{3,1,0,2:T(8,128)}), f32[2,16,8,256]{3,1,0,2:T(8,128)S(1)}, u32[]{:S(2)}, u32[]{:S(2)}) %all-to-all-start.3) | async-done | bytes 262176 | tf_op jit(solution)/shard_map/all_to_all | solution.py:30
  453.2 7.6 %gather_fusion.28 = f32[1024,2,16]{2,1,0:T(2,128)} fusion(f32[2,16,3072]{1,0,2:T(2,128)S(1)} %copy.179, s32[1024]{0:T(1024)} %fusion.109), kind=kCustom, calls=%fused_computation.28.clone | custom fusion | bytes 266240 | tf_op jit(solution)/shard_map/jit(_take)/gather | solution.py:35
  460.8 7.6 %gather_fusion.29 = f32[1024,2,16]{2,1,0:T(2,128)} fusion(f32[2,16,3072]{1,0,2:T(2,128)S(1)} %copy.179, s32[1024]{0:T(1024)} %fusion.110), kind=kCustom, calls=%fused_computation.29.clone | custom fusion | bytes 266240 | tf_op jit(solution)/shard_map/jit(_take)/gather | solution.py:35
  468.4 7.6 %gather_fusion.30 = f32[1024,2,16]{2,1,0:T(2,128)} fusion(f32[2,16,3072]{1,0,2:T(2,128)S(1)} %copy.179, s32[1024]{0:T(1024)} %fusion.111), kind=kCustom, calls=%fused_computation.30.clone | custom fusion | bytes 266240 | tf_op jit(solution)/shard_map/jit(_take)/gather | solution.py:35
  476.0 7.6 %gather_fusion.31 = f32[1024,2,16]{2,1,0:T(2,128)} fusion(f32[2,16,3072]{1,0,2:T(2,128)S(1)} %copy.179, s32[1024]{0:T(1024)} %fusion.112), kind=kCustom, calls=%fused_computation.31.clone | custom fusion | bytes 266240 | tf_op jit(solution)/shard_map/jit(_take)/gather | solution.py:35
  483.6 7.5 %gather_fusion.32 = f32[1024,2,16]{2,1,0:T(2,128)} fusion(f32[2,16,3072]{1,0,2:T(2,128)S(1)} %copy.179, s32[1024]{0:T(1024)S(1)} %copy-done.29), kind=kCustom, calls=%fused_computation.32.clone | custom fusion | bytes 266240 | tf_op jit(solution)/shard_map/jit(_take)/gather | solution.py:35
  491.1 7.5 %gather_fusion.33 = f32[1024,2,16]{2,1,0:T(2,128)} fusion(f32[2,16,3072]{1,0,2:T(2,128)S(1)} %copy.179, s32[1024]{0:T(1024)S(1)} %copy-done.28), kind=kCustom, calls=%fused_computation.33.clone | custom fusion | bytes 266240 | tf_op jit(solution)/shard_map/jit(_take)/gather | solution.py:35
  498.6 7.5 %gather_fusion.34 = f32[1024,2,16]{2,1,0:T(2,128)} fusion(f32[2,16,3072]{1,0,2:T(2,128)S(1)} %copy.179, s32[1024]{0:T(1024)S(1)} %fusion.115), kind=kCustom, calls=%fused_computation.34.clone | custom fusion | bytes 266240 | tf_op jit(solution)/shard_map/jit(_take)/gather | solution.py:35
  506.1 7.5 %gather_fusion.35 = f32[1024,2,16]{2,1,0:T(2,128)} fusion(f32[2,16,3072]{1,0,2:T(2,128)S(1)} %copy.179, s32[1024]{0:T(1024)S(1)} %fusion.116), kind=kCustom, calls=%fused_computation.35.clone | custom fusion | bytes 266240 | tf_op jit(solution)/shard_map/jit(_take)/gather | solution.py:35
  (198 shorter events, 118.8 us)
Async XLA Ops:
  0.7 27.7 %copy-start.35 = (pred[2048]{0:T(1024)(128)(4,1)}, pred[2048]{0:T(1024)(128)(4,1)S(1)}, u32[]{:S(2)}) copy-start(pred[2048]{0:T(1024)(128)(4,1)S(1)} %compare_and_fusion) | copy-start | bytes 6148
  16.5 17.1 %copy-start = (f32[2,16,1024]{2,1,0:T(8,128)S(1)}, f32[2,16,1024]{2,1,0:T(8,128)}, u32[]{:S(2)}) copy-start(f32[2,16,1024]{2,1,0:T(8,128)} %param.10) | copy-start | bytes 393220
  16.5 17.1 %copy-start.39 = (s32[8,1024]{1,0:T(8,128)S(1)}, s32[8,1024]{1,0:T(8,128)}, u32[]{:S(2)}) copy-start(s32[8,1024]{1,0:T(8,128)} %param.15) | copy-start | bytes 98308
  16.5 23.1 %copy-start.34 = (f32[2,8,1024]{2,1,0:T(8,128)S(1)}, f32[2,8,1024]{2,1,0:T(8,128)}, u32[]{:S(2)}) copy-start(f32[2,8,1024]{2,1,0:T(8,128)} %param.11) | copy-start | bytes 196612
  26.5 37.2 %copy-start.41 = (f32[1024]{0:T(1024)S(1)}, f32[1024]{0:T(1024)}, u32[]{:S(2)}) copy-start(f32[1024]{0:T(1024)} %param.13) | copy-start | bytes 12292
  26.6 38.5 %copy-start.40 = (f32[8,1024]{1,0:T(8,128)S(1)}, f32[8,1024]{1,0:T(8,128)}, u32[]{:S(2)}) copy-start(f32[8,1024]{1,0:T(8,128)} %param.12) | copy-start | bytes 98308
  28.5 37.2 %all-to-all-start = ((f32[2,16,8,256]{3,1,0,2:T(8,128)}), f32[2,16,8,256]{3,1,0,2:T(8,128)S(1)}, u32[]{:S(2)}, u32[]{:S(2)}) async-start(f32[2,16,8,256]{3,1,0,2:T(8,128)} %copy.120), calls=%async_computation | async-start | bytes 524288 | tf_op jit(solution)/shard_map/all_to_all | solution.py:30
  146.6 27.1 %copy-start.36 = (pred[2048]{0:T(1024)(128)(4,1)S(1)}, pred[2048]{0:T(1024)(128)(4,1)}, u32[]{:S(2)}) copy-start(pred[2048]{0:T(1024)(128)(4,1)} %copy-done.35) | copy-start | bytes 6148
  148.4 0.6 copy-start.11
  148.5 0.6 copy-start.13
  185.6 10.3 %all-to-all-start.1 = ((f32[2,16,8,256]{3,1,0,2:T(8,128)}), f32[2,16,8,256]{3,1,0,2:T(8,128)S(1)}, u32[]{:S(2)}, u32[]{:S(2)}) async-start(f32[2,16,8,256]{3,1,0,2:T(8,128)} %copy.139), calls=%async_computation.1 | async-start | bytes 524288 | tf_op jit(solution)/shard_map/all_to_all | solution.py:30
  261.4 10.4 %copy-start.9 = (f32[1024,2,16]{2,1,0:T(2,128)S(1)}, f32[1024,2,16]{2,1,0:T(2,128)}, u32[]{:S(2)}) copy-start(f32[1024,2,16]{2,1,0:T(2,128)} %gather_fusion.15) | copy-start | bytes 393220
  263.5 9.3 %copy-start.7 = (f32[1024,2,16]{2,1,0:T(2,128)S(1)}, f32[1024,2,16]{2,1,0:T(2,128)}, u32[]{:S(2)}) copy-start(f32[1024,2,16]{2,1,0:T(2,128)} %gather_fusion.16) | copy-start | bytes 393220
  265.6 7.6 %copy-start.5 = (f32[1024,2,16]{2,1,0:T(2,128)S(1)}, f32[1024,2,16]{2,1,0:T(2,128)}, u32[]{:S(2)}) copy-start(f32[1024,2,16]{2,1,0:T(2,128)} %gather_fusion.17) | copy-start | bytes 393220
  273.3 26.6 %copy-start.37 = (pred[2048]{0:T(1024)(128)(4,1)S(1)}, pred[2048]{0:T(1024)(128)(4,1)}, u32[]{:S(2)}) copy-start(pred[2048]{0:T(1024)(128)(4,1)} %copy-done.35) | copy-start | bytes 6148
  275.5 0.6 copy-start.15
  275.5 0.6 copy-start.17
  311.7 10.3 %all-to-all-start.2 = ((f32[2,16,8,256]{3,1,0,2:T(8,128)}), f32[2,16,8,256]{3,1,0,2:T(8,128)S(1)}, u32[]{:S(2)}, u32[]{:S(2)}) async-start(f32[2,16,8,256]{3,1,0,2:T(8,128)} %copy.158), calls=%async_computation.2 | async-start | bytes 524288 | tf_op jit(solution)/shard_map/all_to_all | solution.py:30
  387.6 10.4 %copy-start.10 = (f32[1024,2,16]{2,1,0:T(2,128)S(1)}, f32[1024,2,16]{2,1,0:T(2,128)}, u32[]{:S(2)}) copy-start(f32[1024,2,16]{2,1,0:T(2,128)} %gather_fusion.24) | copy-start | bytes 393220
  389.7 9.3 %copy-start.8 = (f32[1024,2,16]{2,1,0:T(2,128)S(1)}, f32[1024,2,16]{2,1,0:T(2,128)}, u32[]{:S(2)}) copy-start(f32[1024,2,16]{2,1,0:T(2,128)} %gather_fusion.25) | copy-start | bytes 393220
  391.8 7.6 %copy-start.6 = (f32[1024,2,16]{2,1,0:T(2,128)S(1)}, f32[1024,2,16]{2,1,0:T(2,128)}, u32[]{:S(2)}) copy-start(f32[1024,2,16]{2,1,0:T(2,128)} %gather_fusion.26) | copy-start | bytes 393220
  399.4 26.6 %copy-start.38 = (pred[2048]{0:T(1024)(128)(4,1)S(1)}, pred[2048]{0:T(1024)(128)(4,1)}, u32[]{:S(2)}) copy-start(pred[2048]{0:T(1024)(128)(4,1)} %copy-done.35) | copy-start | bytes 6148
  401.7 0.6 copy-start.19
  401.7 0.6 copy-start.21
  437.8 45.7 %copy-start.29 = (s32[1024]{0:T(1024)S(1)}, s32[1024]{0:T(1024)}, u32[]{:S(2)}) copy-start(s32[1024]{0:T(1024)} %fusion.113) | copy-start | bytes 12292
  437.8 10.4 %all-to-all-start.3 = ((f32[2,16,8,256]{3,1,0,2:T(8,128)}), f32[2,16,8,256]{3,1,0,2:T(8,128)S(1)}, u32[]{:S(2)}, u32[]{:S(2)}) async-start(f32[2,16,8,256]{3,1,0,2:T(8,128)} %copy.177), calls=%async_computation.3 | async-start | bytes 524288 | tf_op jit(solution)/shard_map/all_to_all | solution.py:30
  441.6 49.5 %copy-start.28 = (s32[1024]{0:T(1024)S(1)}, s32[1024]{0:T(1024)}, u32[]{:S(2)}) copy-start(s32[1024]{0:T(1024)} %fusion.114) | copy-start | bytes 12292
  513.6 6.2 %copy-start.1 = (f32[1024,2,16]{2,1,0:T(2,128)S(1)}, f32[1024,2,16]{2,1,0:T(2,128)}, u32[]{:S(2)}) copy-start(f32[1024,2,16]{2,1,0:T(2,128)} %gather_fusion.31) | copy-start | bytes 393220
  513.6 7.3 %copy-start.2 = (f32[1024,2,16]{2,1,0:T(2,128)S(1)}, f32[1024,2,16]{2,1,0:T(2,128)}, u32[]{:S(2)}) copy-start(f32[1024,2,16]{2,1,0:T(2,128)} %gather_fusion.32) | copy-start | bytes 393220
  513.6 8.4 %copy-start.3 = (f32[1024,2,16]{2,1,0:T(2,128)S(1)}, f32[1024,2,16]{2,1,0:T(2,128)}, u32[]{:S(2)}) copy-start(f32[1024,2,16]{2,1,0:T(2,128)} %gather_fusion.33) | copy-start | bytes 393220
  519.8 5.2 copy-start.30
  519.8 5.2 copy-start.31
  519.8 5.2 copy-start.32
  519.8 5.2 copy-start.33
  520.9 3.6 copy-start.4
  522.0 3.0 copy-start.20
  522.0 3.0 copy-start.22
  522.0 3.0 copy-start.23
  522.0 3.0 copy-start.24
  522.0 3.0 copy-start.25
  522.0 3.0 copy-start.26
  522.0 3.0 copy-start.27
  522.0 4.5 copy-start.12
  522.1 4.5 copy-start.14
  522.1 4.5 copy-start.16
  522.1 4.5 copy-start.18
